TPU v7x, 256 devices: a whole 4x4x8 slice. The times are simulated.
256 devices in a mesh: ctx: 32 (over x, y, core), ch: 8 (over z).
Axes of the slice: x: 4, y: 4, z: 8, core: 2. Of those that a mesh axis runs over, the one named last changes fastest.
Arguments:
- gate_input: bfloat16 [8192, 16384], P('ch', 'ctx'), may hold values from -90 to 90
- key_input: bfloat16 [8192, 16384], P('ch', 'ctx'), may hold values from -6 to 6
- value_input: bfloat16 [8192, 16384], P('ch', 'ctx'), may hold values from -6 to 6
- short_filter: float32 [3, 3, 8192], P(None, None, 'ch'), may hold values from -3.5 to 3.5
- mr_filter: float32 [512, 128], P('ch'), may hold values from -0.5 to 0.5
- mr_skip: float32 [8192], P('ch'), may hold values from -3 to 3
- norm_gain: float32 [8192], P('ch'), may hold values from 0.5 to 1.5
- doc_lengths: int32 [64], replicated, may hold values from 1 to 2048, 16384 in all
Outputs:
- relaid: bfloat16 [8192, 16384], P(('ch', 'ctx'))
Inputs may be any that keep to these rules, and one draw needn't show every extreme that they name: `doc_lengths`: the 64 lengths sum to 16384, and one of them is exactly 2048.
All inputs are finite; a program needn't handle non-finite values.
Results may differ from a plain program's by a relative error of at most 0.0095.
Values may be sent and summed in bfloat16 or wider, within the bound.
No kernel may reach another device: no remote copies, remote signals or barrier semaphores. Data moves between devices by JAX's collectives and lax.ppermute only.
A program may use at most 128 MiB of HBM per device.

v0:
```python
import math
import jax
import jax.numpy as jnp
from jax import lax
from jax.sharding import PartitionSpec as P

D = 8192
GROUP = 16
SHORT = 3
MR = 128
NORM_EPS = 1e-06


def doc_starts(doc_lengths, positions):
    doc_ends = jnp.cumsum(doc_lengths)
    doc_firsts = doc_ends - doc_lengths
    before_row = doc_firsts[:, None] <= positions[None, :]
    return jnp.max(jnp.where(before_row, doc_firsts[:, None], 0), axis=0)


def short_conv(raw_rows, prior_rows, tap_rows, positions, starts):
    row_count = raw_rows.shape[1]
    extended = jnp.concatenate([prior_rows, raw_rows], axis=1).astype(jnp.float32)
    running = jnp.zeros(raw_rows.shape, jnp.float32)
    for tap_lag in range(SHORT):
        lagged = lax.slice_in_dim(
            extended, SHORT - 1 - tap_lag, SHORT - 1 - tap_lag + row_count, axis=1
        )
        in_document = positions - tap_lag >= starts
        running = running + jnp.where(
            in_document[None, :], tap_rows[tap_lag][:, None] * lagged, 0.0
        )
    return running


def features(raw_list, prior_list, short_taps, positions, starts):
    gate_conv = short_conv(raw_list[0], prior_list[0], short_taps[0], positions, starts)
    key_conv = short_conv(raw_list[1], prior_list[1], short_taps[1], positions, starts)
    value_conv = short_conv(raw_list[2], prior_list[2], short_taps[2], positions, starts)
    return (gate_conv, (key_conv * value_conv).astype(jnp.bfloat16))


def toeplitz(taps_bf):
    groups = taps_bf.shape[0]
    padded = jnp.concatenate(
        [jnp.zeros((groups, MR), jnp.bfloat16), taps_bf, jnp.zeros((groups, MR + 1), jnp.bfloat16)],
        axis=1,
    )
    repeated = jnp.tile(padded, (1, 2 * MR))[:, : 2 * MR * 3 * MR].reshape(groups, 2 * MR, 3 * MR)
    return repeated[:, :, 2 * MR :]


def long_conv(values, prior_rows, taps_bf, starts):
    channels, row_count = values.shape
    groups = taps_bf.shape[0]
    members = channels // groups
    tile_count = row_count // MR
    blocked = jnp.concatenate([prior_rows, values], axis=1).reshape(channels, tile_count + 1, MR)
    windows = jnp.concatenate([blocked[:, :-1], blocked[:, 1:]], axis=2).reshape(
        groups, members, tile_count, 2 * MR
    )
    matrices = toeplitz(taps_bf)
    per_step = math.gcd(tile_count, max(1, 64 // groups))
    tile_starts = starts.reshape(tile_count, MR)
    source_offsets = jnp.arange(2 * MR, dtype=jnp.int32) - MR
    step_offsets = jnp.arange(per_step, dtype=jnp.int32) * MR
    zero_bf = jnp.zeros((), jnp.bfloat16)

    def advance(step_index, result):
        block_begin = step_index * per_step
        window_part = lax.dynamic_slice_in_dim(windows, block_begin, per_step, axis=2)
        row_starts = lax.dynamic_slice_in_dim(tile_starts, block_begin, per_step, axis=0)
        tile_first = block_begin * MR + step_offsets
        sources = tile_first[:, None] + source_offsets[None, :]
        allowed = sources[:, :, None] >= row_starts[:, None, :]
        masked = jnp.where(allowed[:, None], matrices[None], zero_bf)
        product = jnp.einsum(
            "gcns,ngst->gcnt", window_part, masked, preferred_element_type=jnp.float32
        )
        return lax.dynamic_update_slice_in_dim(result, product, block_begin, axis=2)

    result = lax.fori_loop(
        0,
        tile_count // per_step,
        advance,
        jnp.zeros((groups, members, tile_count, MR), jnp.float32),
    )
    return result.reshape(channels, row_count)


def row_total(partial_value):
    return lax.psum(partial_value, "ch")


def local(
    gate_input, key_input, value_input, short_filter, mr_filter, mr_skip, norm_gain, doc_lengths
):
    ctx_place = lax.axis_index("ctx")
    stacked = jnp.stack([gate_input, key_input, value_input])
    received = lax.all_to_all(stacked, "ctx", split_axis=1, concat_axis=2, tiled=True)
    narrow = received.shape[1]
    all_rows = received.shape[2]
    chan_offset = ctx_place * narrow
    positions = jnp.arange(all_rows, dtype=jnp.int32)
    starts = doc_starts(doc_lengths, positions)
    short_taps = lax.dynamic_slice_in_dim(short_filter, chan_offset, narrow, axis=2)
    zero_prior = jnp.zeros((narrow, SHORT - 1), jnp.bfloat16)
    gate_conv, product_rows = features(
        [received[0], received[1], received[2]],
        [zero_prior, zero_prior, zero_prior],
        short_taps,
        positions,
        starts,
    )
    group_rows = lax.dynamic_slice_in_dim(
        mr_filter, chan_offset // GROUP, max(1, narrow // GROUP), axis=0
    )
    skip_here = lax.dynamic_slice_in_dim(mr_skip, chan_offset, narrow)
    gain_here = lax.dynamic_slice_in_dim(norm_gain, chan_offset, narrow)
    zero_rows = jnp.zeros((narrow, MR), jnp.bfloat16)
    mixed_rows = long_conv(
        product_rows, zero_rows, group_rows.astype(jnp.bfloat16), starts
    ) + skip_here[:, None] * product_rows.astype(jnp.float32)
    gated = gate_conv * mixed_rows
    shares = lax.psum_scatter(
        jnp.sum(gated * gated, axis=0).astype(jnp.bfloat16), "ctx", scatter_dimension=0, tiled=True
    ).astype(jnp.float32)
    own_scale = lax.rsqrt(row_total(shares) / D + NORM_EPS)
    row_scale = lax.all_gather(own_scale, "ctx", axis=0, tiled=True)
    return (gated * row_scale[None, :] * gain_here[:, None]).astype(jnp.bfloat16)


def solution(mesh):
    in_specs = (
        P("ch", "ctx"),
        P("ch", "ctx"),
        P("ch", "ctx"),
        P(None, None, "ch"),
        P("ch", None),
        P("ch"),
        P("ch"),
        P(),
    )
    out_specs = P(("ch", "ctx"), None)
    return jax.shard_map(local, mesh=mesh, in_specs=in_specs, out_specs=out_specs, check_vma=False)
```

profile of v0, /device:TPU:1, one launch (start us, length us, event | category | flops | bytes accessed | tf_op | source)
XLA Modules:
  0.0 279.0 jit_solution(16619326890867095155)
XLA Ops:
  0.0 2.2 pad_maximum_fusion
  2.2 4.7 %copy.30 = bf16[3,1024,512]{2,0,1:T(4,128)(2,1)} copy(bf16[3,1024,512]{2,1,0:T(8,128)(2,1)S(1)} %pad_maximum_fusion) | data formatting | bytes 6291456 | tf_op jit(solution)/shard_map/stack | solution.py:99
  6.9 8.8 %all-to-all-start = ((bf16[3,1024,512]{2,0,1:T(4,128)(2,1)}), bf16[3,1024,512]{2,0,1:T(4,128)(2,1)}, u32[]{:S(2)}, u32[]{:S(2)}) async-start(bf16[3,1024,512]{2,0,1:T(4,128)(2,1)} %copy.30), calls=%async_computation | async-start | bytes 8388608 | tf_op jit(solution)/shard_map/all_to_all | solution.py:100
  16.2 1.3 tile.10
  22.3 45.5 %all-to-all-done = bf16[3,1024,512]{2,0,1:T(4,128)(2,1)} async-done(((bf16[3,1024,512]{2,0,1:T(4,128)(2,1)}), bf16[3,1024,512]{2,0,1:T(4,128)(2,1)}, u32[]{:S(2)}, u32[]{:S(2)}) %all-to-all-start) | async-done | bytes 3145760 | tf_op jit(solution)/shard_map/all_to_all | solution.py:100
  67.9 11.2 %fusion.39 = (bf16[1,32,32,512]{3,0,1,2:T(2,128)(2,1)}, bf16[1,32,32,512]{3,0,1,2:T(2,128)(2,1)S(1)}, bf16[1,32,32,512]{3,0,1,2:T(2,128)(2,1)S(1)}) fusion(bf16[3,32,32,512]{3,0,1,2:T(4,128)(2,1)} %bitcast.6), kind=kLoop, calls=%fused_computation.77 | loop fusion | bytes 6291456 | tf_op jit(solution)/shard_map/slice | solution.py:109
  83.2 2.4 fusion.18
  87.1 1.6 broadcast_in_dim.159.clone
  88.7 15.0 %while.16 = (s32[]{:T(128)}, f32[2,16,128,128]{3,2,1,0:T(8,128)}, s32[128,128]{1,0:T(8,128)S(1)}, bf16[2,256,128]{2,1,0:T(8,128)(2,1)S(1)}, bf16[2,16,128,256]{3...) while((s32[]{:T(128)}, f32[2,16,128,128]{3,2,1,0:T(8,128)}, ...), condition=%wide.region_3.4_spmd.clone, body=%wide.region_2.3_spmd.clone.sunk | while | flops 70263112 | bytes 5491127 | solution.py:82
  88.8 1.4 broadcast_compare_fusion.2
  90.3 1.2 fusion.46
  92.5 1.4 broadcast_compare_fusion.2
  94.0 1.2 fusion.46
  96.3 1.4 broadcast_compare_fusion.2
  97.7 1.2 fusion.46
  100.0 1.4 broadcast_compare_fusion.2
  101.5 1.2 fusion.46
  103.7 2.7 copy.31
  107.4 1.2 copy-done.1
  108.6 2.3 multiply_reduce_fusion
  110.9 120.1 %all-reduce.4 = bf16[16384]{0:T(1024)(128)(2,1)S(1)} all-reduce(bf16[16384]{0:T(1024)(128)(2,1)S(1)} %get-tuple-element.225), channel_id=2, replica_groups=mesh['ctx'=32,'ch'=8] {'ctx'}, use_global_device_ids=true, to_apply=%region_5.6.clone | all-reduce | flops 16384 | bytes 65536
  231.1 16.5 %psum.7 = f32[512]{0:T(512)S(1)} all-reduce(f32[512]{0:T(512)S(1)} %dynamic-slice_convert_fusion), channel_id=1, replica_groups=mesh['ctx'=32,'ch'=8] {'ch'}, use_global_device_ids=true, to_apply=%region_6.7 | all-reduce | flops 512 | bytes 4096 | tf_op jit(solution)/shard_map/psum | solution.py:92
  247.6 30.2 %all-gather = f32[32,1,512]{2,1,0:T(1,128)S(1)} all-gather(f32[1,1,512]{2,1,0:T(1,128)S(1)} %bitcast.69), channel_id=1, replica_groups=mesh['ctx'=32,'ch'=8] {'ctx'}, dimensions={0}, use_global_device_ids=true | all-gather | bytes 67584 | tf_op jit(solution)/shard_map/all_gather | solution.py:129
  277.8 1.2 multiply_convert_fusion
  (64 shorter events, 15.7 us)
Async XLA Ops:
  0.0 16.1 %copy-start = (f32[64,128]{1,0:T(8,128)S(1)}, f32[64,128]{1,0:T(8,128)}, u32[]{:S(2)}) copy-start(f32[64,128]{1,0:T(8,128)} %param.14) | copy-start | bytes 98308
  6.9 8.8 %copy-start.2 = (s32[64]{0:T(128)S(1)}, s32[64]{0:T(128)}, u32[]{:S(2)}) copy-start(s32[64]{0:T(128)} %param.17) | copy-start | bytes 772
  6.9 61.0 %all-to-all-start = ((bf16[3,1024,512]{2,0,1:T(4,128)(2,1)}), bf16[3,1024,512]{2,0,1:T(4,128)(2,1)}, u32[]{:S(2)}, u32[]{:S(2)}) async-start(bf16[3,1024,512]{2,0,1:T(4,128)(2,1)} %copy.30), calls=%async_computation | async-start | bytes 8388608 | tf_op jit(solution)/shard_map/all_to_all | solution.py:100
  15.7 3.7 %copy-start.3 = (u32[256]{0:T(256)S(1)}, u32[256]{0:T(256)}, u32[]{:S(2)}) copy-start(u32[256]{0:T(256)} %constant.121) | copy-start | bytes 3076
  107.0 1.6 copy-start.1
where the time goes:
time: 279 us
  blocking collectives  167 us (60%)
  waiting for transfers between devices  45.5 us (16%)
  local copies, waits for them, and re-layouts  35.5 us (13%)
  other arithmetic  16.6 us (6%)
  starting transfers between devices  8.79 us (3%)
  matrix products  4.89 us (2%)
    unnamed x1, blocking collectives  120 us
    all_to_all x1, waiting for transfers between devices, local(): lax.all_to_all(stacked, 'ctx', split_axis=1, concat_axis=2, tiled=True)  45.5 us
    all_gather x1, blocking collectives, local(): row_scale = lax.all_gather(own_scale, 'ctx', axis=0, tiled=True)  30.2 us
    psum x1, blocking collectives, row_total(): return lax.psum(partial_value, 'ch')  16.5 us
    slice x2, local copies, waits for them, and re-layouts, local(): received[0]  13.9 us
    all_to_all x1, starting transfers between devices, local(): lax.all_to_all(stacked, 'ctx', split_axis=1, concat_axis=2, tiled=True)  8.79 us
  transfers between devices with their start and end apart: 1, of which 1 were waited for; matrix products, arithmetic and copies ran while one was open for 2% of the time, Pallas kernels for 0%

commit v1 on v0

--- a/solution.py
+++ b/solution.py
@@ -9,6 +9,11 @@
 SHORT = 3
 MR = 128
 NORM_EPS = 1e-06
+
+
+def masks_close(incoming_x):
+    state_next = jnp.sum(lax.all_gather(incoming_x, "ch"), axis=0)
+    return state_next
 
 
 def doc_starts(doc_lengths, positions):
@@ -89,7 +94,7 @@
 
 
 def row_total(partial_value):
-    return lax.psum(partial_value, "ch")
+    return masks_close(partial_value)
 
 
 def local(

time: 279 us -> 285 us (1.022)
  blocking collectives: 167 us -> 172 us
    all_gather x0 -> x1, blocking collectives: none -> 19.9 us  [masks_close(): state_next = jnp.sum(lax.all_gather(incoming_x, 'ch'), axis=0)]
    psum x1 -> x0, blocking collectives: 16.5 us -> none  [row_total(): return lax.psum(partial_value, 'ch')]
where the time goes in v1:
time: 285 us; the launch traced here: 284 us
  blocking collectives  172 us (60%)
  waiting for transfers between devices  45.5 us (16%)
  local copies, waits for them, and re-layouts  35.5 us (12%)
  other arithmetic  16.6 us (6%)
  starting transfers between devices  8.79 us (3%)
  matrix products  4.89 us (2%)
    unnamed x1, blocking collectives  120 us
    all_to_all x1, waiting for transfers between devices, local(): lax.all_to_all(stacked, 'ctx', split_axis=1, concat_axis=2, tiled=True)  45.5 us
    all_gather x1, blocking collectives, local(): row_scale = lax.all_gather(own_scale, 'ctx', axis=0, tiled=True)  32.1 us
    all_gather x1, blocking collectives, masks_close(): state_next = jnp.sum(lax.all_gather(incoming_x, 'ch'), axis=0)  19.9 us
    slice x2, local copies, waits for them, and re-layouts, local(): received[0]  13.9 us
    all_to_all x1, starting transfers between devices, local(): lax.all_to_all(stacked, 'ctx', split_axis=1, concat_axis=2, tiled=True)  8.79 us
  transfers between devices with their start and end apart: 1, of which 1 were waited for; matrix products, arithmetic and copies ran while one was open for 2% of the time, Pallas kernels for 0%

profile of v1, /device:TPU:1, one launch (start us, length us, event | category | flops | bytes accessed | tf_op | source)
XLA Modules:
  0.0 284.4 jit_solution(4545439141907128054)
XLA Ops:
  0.0 2.2 pad_maximum_fusion
  2.2 4.7 %copy.30 = bf16[3,1024,512]{2,0,1:T(4,128)(2,1)} copy(bf16[3,1024,512]{2,1,0:T(8,128)(2,1)S(1)} %pad_maximum_fusion) | data formatting | bytes 6291456 | tf_op jit(solution)/shard_map/stack | solution.py:104
  6.9 8.8 %all-to-all-start = ((bf16[3,1024,512]{2,0,1:T(4,128)(2,1)}), bf16[3,1024,512]{2,0,1:T(4,128)(2,1)}, u32[]{:S(2)}, u32[]{:S(2)}) async-start(bf16[3,1024,512]{2,0,1:T(4,128)(2,1)} %copy.30), calls=%async_computation | async-start | bytes 8388608 | tf_op jit(solution)/shard_map/all_to_all | solution.py:105
  16.2 1.3 tile.10
  22.3 45.5 %all-to-all-done = bf16[3,1024,512]{2,0,1:T(4,128)(2,1)} async-done(((bf16[3,1024,512]{2,0,1:T(4,128)(2,1)}), bf16[3,1024,512]{2,0,1:T(4,128)(2,1)}, u32[]{:S(2)}, u32[]{:S(2)}) %all-to-all-start) | async-done | bytes 3145760 | tf_op jit(solution)/shard_map/all_to_all | solution.py:105
  67.9 11.2 %fusion.39 = (bf16[1,32,32,512]{3,0,1,2:T(2,128)(2,1)}, bf16[1,32,32,512]{3,0,1,2:T(2,128)(2,1)S(1)}, bf16[1,32,32,512]{3,0,1,2:T(2,128)(2,1)S(1)}) fusion(bf16[3,32,32,512]{3,0,1,2:T(4,128)(2,1)} %bitcast.6), kind=kLoop, calls=%fused_computation.77 | loop fusion | bytes 6291456 | tf_op jit(solution)/shard_map/slice | solution.py:114
  83.2 2.4 fusion.18
  87.1 1.6 broadcast_in_dim.159.clone
  88.7 15.0 %while.16 = (s32[]{:T(128)}, f32[2,16,128,128]{3,2,1,0:T(8,128)}, s32[128,128]{1,0:T(8,128)S(1)}, bf16[2,256,128]{2,1,0:T(8,128)(2,1)S(1)}, bf16[2,16,128,256]{3...) while((s32[]{:T(128)}, f32[2,16,128,128]{3,2,1,0:T(8,128)}, ...), condition=%wide.region_3.4_spmd.clone, body=%wide.region_2.3_spmd.clone.sunk | while | flops 70263112 | bytes 5491127 | solution.py:87
  88.8 1.4 broadcast_compare_fusion.2
  90.3 1.2 fusion.46
  92.5 1.4 broadcast_compare_fusion.2
  94.0 1.2 fusion.46
  96.3 1.4 broadcast_compare_fusion.2
  97.7 1.2 fusion.46
  100.0 1.4 broadcast_compare_fusion.2
  101.5 1.2 fusion.46
  103.7 2.7 copy.31
  107.4 1.2 copy-done.1
  108.6 2.3 multiply_reduce_fusion
  110.9 120.1 %all-reduce.4 = bf16[16384]{0:T(1024)(128)(2,1)S(1)} all-reduce(bf16[16384]{0:T(1024)(128)(2,1)S(1)} %get-tuple-element.225), channel_id=3, replica_groups=mesh['ctx'=32,'ch'=8] {'ctx'}, use_global_device_ids=true, to_apply=%region_5.6.clone | all-reduce | flops 16384 | bytes 65536
  231.1 19.9 %all-gather.1 = f32[8,1,512]{2,1,0:T(1,128)S(1)} all-gather(f32[1,1,512]{2,1,0:T(1,128)S(1)} %bitcast.70), channel_id=2, replica_groups=mesh['ctx'=32,'ch'=8] {'ch'}, dimensions={0}, use_global_device_ids=true | all-gather | bytes 18432 | tf_op jit(solution)/shard_map/all_gather | solution.py:15
  251.1 32.1 %all-gather.2 = f32[32,1,512]{2,1,0:T(1,128)S(1)} all-gather(f32[1,1,512]{2,1,0:T(1,128)S(1)} %bitcast.71), channel_id=1, replica_groups=mesh['ctx'=32,'ch'=8] {'ctx'}, dimensions={0}, use_global_device_ids=true | all-gather | bytes 67584 | tf_op jit(solution)/shard_map/all_gather | solution.py:134
  283.2 1.2 multiply_convert_fusion
  (65 shorter events, 15.7 us)
Async XLA Ops:
  0.0 16.1 %copy-start = (f32[64,128]{1,0:T(8,128)S(1)}, f32[64,128]{1,0:T(8,128)}, u32[]{:S(2)}) copy-start(f32[64,128]{1,0:T(8,128)} %param.14) | copy-start | bytes 98308
  6.9 8.8 %copy-start.2 = (s32[64]{0:T(128)S(1)}, s32[64]{0:T(128)}, u32[]{:S(2)}) copy-start(s32[64]{0:T(128)} %param.17) | copy-start | bytes 772
  6.9 61.0 %all-to-all-start = ((bf16[3,1024,512]{2,0,1:T(4,128)(2,1)}), bf16[3,1024,512]{2,0,1:T(4,128)(2,1)}, u32[]{:S(2)}, u32[]{:S(2)}) async-start(bf16[3,1024,512]{2,0,1:T(4,128)(2,1)} %copy.30), calls=%async_computation | async-start | bytes 8388608 | tf_op jit(solution)/shard_map/all_to_all | solution.py:105
  15.7 3.7 %copy-start.3 = (u32[256]{0:T(256)S(1)}, u32[256]{0:T(256)}, u32[]{:S(2)}) copy-start(u32[256]{0:T(256)} %constant.121) | copy-start | bytes 3076
  107.0 1.6 copy-start.1
